TPU v7x, 32 devices: a whole 2x2x4 slice. The times are simulated.
32 devices in a mesh: groups: 2 (over x), row: 2 (over core), col: 8 (over z, y).
Axes of the slice: x: 2, y: 2, z: 4, core: 2. Of those that a mesh axis runs over, the one named last changes fastest.
Arguments:
- pair: bfloat16 [1280, 640, 128], P(('groups', 'col'), 'row'), parts along dimension 0, may hold values from -6 to 6
- token_mask: int32 [1280], P('groups'), parts along dimension 0, may hold values 0 or 1
- start_gain: float32 [128], replicated, may hold values from 0.25 to 1.75
- start_head_gain: float32 [128], replicated, may hold values from 0.25 to 1.75
- start_in: bfloat16 [128, 512], replicated, may hold values from -0.5 to 0.5
- start_out: bfloat16 [128, 128], replicated, may hold values from -0.5 to 0.5
- end_gain: float32 [128], replicated, may hold values from 0.25 to 1.75
- end_head_gain: float32 [128], replicated, may hold values from 0.25 to 1.75
- end_in: bfloat16 [128, 512], replicated, may hold values from -0.5 to 0.5
- end_out: bfloat16 [128, 128], replicated, may hold values from -0.5 to 0.5
- trans_gain: float32 [128], replicated, may hold values from 0.25 to 1.75
- trans_in: bfloat16 [128, 1024], replicated, may hold values from -0.5 to 0.5
- trans_out: bfloat16 [512, 128], replicated, may hold values from -0.25 to 0.25
Outputs:
- update_start: bfloat16 [1280, 640, 128], P(('groups', 'col'), 'row'), parts along dimension 0
- update_end: bfloat16 [1280, 640, 128], P(('groups', 'col'), 'row'), parts along dimension 0
- update_trans: bfloat16 [1280, 640, 128], P(('groups', 'col'), 'row'), parts along dimension 0
There are 2 independent parts, one for each index of `groups`. A program takes and returns all parts, laid end to end along the dimension named above; an argument that names none is the same for every part. Nothing has to cross between parts.
Inputs may be any that keep to these rules, and one draw needn't show every extreme that they name: `token_mask`: 1 marks a valid token of the complex, 0 a padded one.
All inputs are finite; a program needn't handle non-finite values.
Results may differ from a plain program's by a relative error of at most 0.018.
Values may be sent and summed in bfloat16 or wider, within the bound.
No kernel may reach another device: no remote copies, remote signals or barrier semaphores. Data moves between devices by JAX's collectives and lax.ppermute only.
A program may use at most 192 MiB of HBM per device.

v0:
```python
import math

import jax
import jax.numpy as jnp
from jax import lax
from jax.sharding import PartitionSpec as P

HEADS = 4


EPSILON = 1e-05


def layer_norm(values, scales):
    average = jnp.mean(values, axis=-1, keepdims=True)
    centered = values - average
    variance = jnp.mean(centered * centered, axis=-1, keepdims=True)
    return centered * lax.rsqrt(variance + EPSILON) * scales


def feature(values):
    return jax.nn.elu(values) + 1.0


def key_value(project, pair_valid, width, depth):
    shape = project.shape[:2] + (HEADS, depth)
    key_feat = (
        (feature(project[..., :width]) * pair_valid[..., None]).astype(jnp.bfloat16).reshape(shape)
    )
    values = project[..., width : 2 * width].astype(jnp.bfloat16).reshape(shape)
    return (key_feat, values)


def finish(queries, gating, state, totals, numer_form, denom_form, head_gain, w_out):
    width = gating.shape[-1]
    query_f = queries.astype(jnp.float32)
    numer = jnp.einsum(numer_form, query_f, state)
    denom = jnp.maximum(jnp.einsum(denom_form, query_f, totals), 1.0)
    attended = (numer / denom[..., None]).reshape(gating.shape)
    scaled = attended * lax.rsqrt(jnp.mean(attended * attended, axis=-1, keepdims=True) + EPSILON)
    scaled = (scaled * head_gain * gating).astype(jnp.bfloat16)
    update = jnp.dot(scaled.reshape(-1, width), w_out, preferred_element_type=jnp.float32)
    return update.astype(jnp.bfloat16).reshape(gating.shape)


def shards(
    pair,
    token_mask,
    start_gain,
    start_head_gain,
    start_in,
    start_out,
    end_gain,
    end_head_gain,
    end_in,
    end_out,
    trans_gain,
    trans_in,
    trans_out,
):
    row_count = pair.shape[0]
    col_count = pair.shape[1]
    width = pair.shape[2]
    depth = width // HEADS
    valid = token_mask.astype(jnp.float32)
    row_valid = lax.dynamic_slice_in_dim(valid, lax.axis_index("col") * row_count, row_count)
    col_valid = lax.dynamic_slice_in_dim(valid, lax.axis_index("row") * col_count, col_count)
    pair_valid = row_valid[:, None] * col_valid[None, :]
    head_shape = (row_count, col_count, HEADS, depth)
    anchor = pair.astype(jnp.float32)
    normed = layer_norm(anchor, start_gain).astype(jnp.bfloat16)
    project = jnp.dot(normed.reshape(-1, width), start_in, preferred_element_type=jnp.float32)
    project = project.reshape(row_count, col_count, 4 * width)
    queries = feature(project[..., :width]).astype(jnp.bfloat16).reshape(head_shape)
    key_feat, values = key_value(project[..., width : 3 * width], pair_valid, width, depth)
    gating = jax.nn.sigmoid(project[..., 3 * width :])
    partial_value = jnp.einsum(
        "ijhd,ijhe->ihde", key_feat, values, preferred_element_type=jnp.float32
    )
    key_part = jnp.sum(key_feat, axis=1, dtype=jnp.float32)
    state, totals = (
        lax.psum(partial_value.astype(jnp.bfloat16), "row").astype(jnp.float32),
        lax.psum(key_part.astype(jnp.bfloat16), "row").astype(jnp.float32),
    )
    update_start = finish(
        queries,
        gating,
        state,
        totals,
        "ijhd,ihde->ijhe",
        "ijhd,ihd->ijh",
        start_head_gain,
        start_out,
    )
    first_sum = anchor + update_start.astype(jnp.float32)
    normed = layer_norm(first_sum, end_gain).astype(jnp.bfloat16)
    project = jnp.dot(normed.reshape(-1, width), end_in, preferred_element_type=jnp.float32)
    project = project.reshape(row_count, col_count, 4 * width)
    key_feat, values = key_value(project[..., width : 3 * width], pair_valid, width, depth)
    partial_value = jnp.einsum(
        "ijhd,ijhe->jhde", key_feat, values, preferred_element_type=jnp.float32
    )
    key_part = jnp.sum(key_feat, axis=0, dtype=jnp.float32)
    queries = feature(project[..., :width]).astype(jnp.bfloat16).reshape(head_shape)
    gating = jax.nn.sigmoid(project[..., 3 * width :])
    state, totals = (
        lax.psum(partial_value.astype(jnp.bfloat16), "col").astype(jnp.float32),
        lax.psum(key_part.astype(jnp.bfloat16), "col").astype(jnp.float32),
    )
    update_end = finish(
        queries, gating, state, totals, "ijhd,jhde->ijhe", "ijhd,jhd->ijh", end_head_gain, end_out
    )
    second_sum = first_sum + update_end.astype(jnp.float32)
    hidden_width = trans_out.shape[0]
    row_block = math.gcd(row_count, 8)

    def transition(block):
        normed_block = layer_norm(block, trans_gain).astype(jnp.bfloat16)
        lifted = jnp.dot(normed_block, trans_in, preferred_element_type=jnp.float32)
        hidden = (jax.nn.silu(lifted[:, :hidden_width]) * lifted[:, hidden_width:]).astype(
            jnp.bfloat16
        )
        return jnp.dot(hidden, trans_out, preferred_element_type=jnp.float32).astype(jnp.bfloat16)

    update_trans = lax.map(
        transition, second_sum.reshape(row_count // row_block, row_block * col_count, width)
    )
    update_trans = update_trans.reshape(row_count, col_count, width)
    return (update_start, update_end, update_trans)


def solution(mesh):
    in_specs = (
        P(("groups", "col"), "row", None),
        P("groups"),
        P(),
        P(),
        P(),
        P(),
        P(),
        P(),
        P(),
        P(),
        P(),
        P(),
        P(),
    )
    out_specs = (
        P(("groups", "col"), "row", None),
        P(("groups", "col"), "row", None),
        P(("groups", "col"), "row", None),
    )
    return jax.shard_map(shards, mesh=mesh, in_specs=in_specs, out_specs=out_specs, check_vma=False)
```

profile of v0, /device:TPU:0, one launch (start us, length us, event | category | flops | bytes accessed | tf_op | source)
XLA Modules:
  0.0 753.3 jit_solution(8597856424074216572)
XLA Ops:
  8.1 5.2 convert_reduce_fusion
  13.3 8.5 %fusion.12 = f32[80,320]{1,0:T(8,128)S(1)} fusion(bf16[80,320,128]{2,1,0:T(8,128)(2,1)S(1)} %copy-done.2, f32[80,320]{1,0:T(8,128)S(1)} %broadcast_multiply_fusion.3), kind=kLoop, calls=%fused_computation.36 | loop fusion | flops 13081600 | bytes 6758400 | tf_op jit(solution)/shard_map/reduce_sum | solution.py:17
  22.0 18.3 %fusion.41 = f32[80,320,512]{2,1,0:T(8,128)} fusion(bf16[80,320,128]{2,1,0:T(8,128)(2,1)S(1)} %copy-done.2, f32[128]{0:T(128)S(1)} %copy-done.9, f32[80,320]{1,0:T(8,128)S(1)} %add_rsqrt_fusion.4, f32[80,320]{1,0:T(8,128)S(1)} %broadcast_multiply_fusion.3, bf16[128,512]{1,0:T(8,128)(2,1)S(1)} %copy-done), kind=kOutput, calls=%fused_computation.73 | convolution fusion | flops 3371827200 | bytes 59318784 | tf_op jit(solution)/shard_map/dot_general | solution.py:72
  40.2 17.5 %fusion.54 = (bf16[80,128]{1,0:T(8,128)(2,1)S(1)}, bf16[80,320,128]{2,1,0:T(8,128)(2,1)}, bf16[80,320,128]{2,1,0:T(8,128)(2,1)}) fusion(f32[80,320]{1,0:T(8,128)S(1)} %broadcast_multiply_fusion.1, f32[80,320,512]{2,1,0:T(8,128)} %fusion.41), kind=kLoop, calls=%fused_computation.94 | loop fusion | flops 22927360 | bytes 32890880 | tf_op jit(solution)/shard_map/reduce_sum | solution.py:80
  57.7 9.8 %copy.52 = bf16[80,320,128]{1,2,0:T(8,128)(2,1)} copy(bf16[80,320,128]{2,1,0:T(8,128)(2,1)} %get-tuple-element.53) | data formatting | bytes 13107200 | tf_op jit(solution)/shard_map/convert_element_type | solution.py:28
  67.5 9.8 %copy.53 = bf16[80,320,128]{1,2,0:T(8,128)(2,1)} copy(bf16[80,320,128]{2,1,0:T(8,128)(2,1)} %get-tuple-element.55) | data formatting | bytes 13107200 | tf_op jit(solution)/shard_map/slice | solution.py:30
  77.3 9.8 %convolution_convert_fusion.4 = bf16[80,4,32,32]{3,2,1,0:T(8,128)(2,1)} fusion(bf16[80,320,4,32]{1,3,2,0:T(8,128)(2,1)} %bitcast.96, bf16[80,320,4,32]{1,3,2,0:T(8,128)(2,1)} %bitcast.97), kind=kOutput, calls=%fused_computation.80 | convolution fusion | flops 210042880 | bytes 13762560 | tf_op jit(solution)/shard_map/ijhd,ijhe->ihde/dot_general | solution.py:77
  87.7 13.2 %fusion.21 = bf16[80,320,128]{2,1,0:T(8,128)(2,1)} fusion(f32[80,320,512]{2,1,0:T(8,128)} %fusion.41), kind=kLoop, calls=%fused_computation.45 | loop fusion | flops 16384000 | bytes 19660800 | tf_op jit(solution)/shard_map/convert_element_type | solution.py:74
  101.0 3.9 psum.29
  105.1 10.2 %copy.54 = bf16[80,320,128]{1,2,0:T(8,128)(2,1)} copy(bf16[80,320,128]{2,1,0:T(8,128)(2,1)} %fusion.21) | data formatting | bytes 13107200 | tf_op jit(solution)/shard_map/convert_element_type | solution.py:74
  115.3 4.7 fusion.56
  120.2 12.1 %multiply_reduce_fusion.2 = (f32[80,320]{1,0:T(8,128)S(1)}, f32[80,320,4,32]{1,3,2,0:T(8,128)}) fusion(f32[80,320,4]{1,2,0:T(4,128)S(1)} %fusion.49, bf16[80,4,32,32]{3,2,1,0:T(8,128)(2,1)} %all-reduce.4.cloned.1.call-done, bf16[80,320,4,32]{1,3,2,0:T(8,128)(2,1)} %bitcast.95), kind=kOutput, calls=%fused_computation.33 | convolution fusion | flops 219520000 | bytes 20828160 | tf_op jit(solution)/shard_map/ijhd,ihde->ijhe/dot_general | solution.py:37
  132.3 14.9 %copy.57 = f32[80,320,128]{2,1,0:T(8,128)} copy(f32[80,320,128]{1,2,0:T(8,128)} %bitcast.103) | data formatting | bytes 26214400 | tf_op jit(solution)/shard_map/reshape | solution.py:39
  147.2 9.5 %fusion.37 = bf16[80,320,128]{2,1,0:T(8,128)(2,1)S(1)} fusion(f32[80,320,512]{2,1,0:T(8,128)} %fusion.41, f32[80,320,128]{2,1,0:T(8,128)} %copy.57, f32[128]{0:T(128)S(1)} %copy-done.11, f32[80,320]{1,0:T(8,128)S(1)} %add_rsqrt_fusion.3), kind=kLoop, calls=%fused_computation.68 | loop fusion | flops 22937600 | bytes 32870912 | tf_op jit(solution)/shard_map/convert_element_type | solution.py:41
  156.7 3.8 convolution_convert_fusion.2
  160.5 9.0 %fusion.39 = f32[80,320]{1,0:T(8,128)S(1)} fusion(bf16[80,320,128]{2,1,0:T(8,128)(2,1)} %bitcast.84, bf16[80,320,128]{2,1,0:T(8,128)(2,1)} %param.15), kind=kLoop, calls=%fused_computation.70 | loop fusion | flops 13081600 | bytes 13209600 | tf_op jit(solution)/shard_map/reduce_sum | solution.py:15
  169.6 10.1 %multiply_reduce_fusion.3 = f32[80,320]{1,0:T(8,128)S(1)} fusion(bf16[80,320,128]{2,1,0:T(8,128)(2,1)} %bitcast.85, bf16[80,320,128]{2,1,0:T(8,128)(2,1)} %param.15, f32[80,320]{1,0:T(8,128)S(1)} %broadcast_multiply_fusion.2), kind=kLoop, calls=%fused_computation.67 | loop fusion | flops 19635200 | bytes 13312000 | tf_op jit(solution)/shard_map/reduce_sum | solution.py:17
  179.7 20.7 %fusion.40 = f32[80,320,512]{2,1,0:T(8,128)} fusion(bf16[80,320,128]{2,1,0:T(8,128)(2,1)} %bitcast.86, bf16[80,320,128]{2,1,0:T(8,128)(2,1)S(1)} %bitcast.81, f32[128]{0:T(128)S(1)} %copy-done.10, f32[80,320]{1,0:T(8,128)S(1)} %add_rsqrt_fusion.2, f32[80,320]{1,0:T(8,128)S(1)} %broadcast_multiply_fusion.2, bf16[128,512]{1,0:T(8,128)(2,1)S(1)} %copy-done.5), kind=kOutput, calls=%fused_computation.72 | convolution fusion | flops 3378380800 | bytes 65872384 | tf_op jit(solution)/shard_map/dot_general | solution.py:97
  200.5 17.8 %fusion.52 = (bf16[320,128]{1,0:T(8,128)(2,1)S(1)}, bf16[80,320,128]{2,1,0:T(8,128)(2,1)}, bf16[80,320,128]{2,1,0:T(8,128)(2,1)}) fusion(f32[80,320]{1,0:T(8,128)S(1)} %broadcast_multiply_fusion.1, f32[80,320,512]{2,1,0:T(8,128)} %fusion.40), kind=kLoop, calls=%fused_computation.93 | loop fusion | flops 22896640 | bytes 32952320 | tf_op jit(solution)/shard_map/reduce_sum | solution.py:103
  218.2 12.8 %copy.75 = bf16[80,320,128]{0,2,1:T(8,128)(2,1)} copy(bf16[80,320,128]{2,1,0:T(8,128)(2,1)} %get-tuple-element.51) | data formatting | bytes 13107200 | tf_op jit(solution)/shard_map/reshape | solution.py:28
  231.0 12.8 %copy.76 = bf16[80,320,128]{0,2,1:T(8,128)(2,1)} copy(bf16[80,320,128]{2,1,0:T(8,128)(2,1)} %get-tuple-element.54) | data formatting | bytes 13107200 | tf_op jit(solution)/shard_map/reshape | solution.py:30
  244.6 12.2 %convolution_convert_fusion.3 = bf16[320,4,32,32]{3,2,1,0:T(8,128)(2,1)} fusion(bf16[80,320,4,32]{0,3,2,1:T(8,128)(2,1)} %bitcast.92, bf16[80,320,4,32]{0,3,2,1:T(8,128)(2,1)} %bitcast.93), kind=kOutput, calls=%fused_computation.71 | convolution fusion | flops 211025920 | bytes 15728640 | tf_op jit(solution)/shard_map/ijhd,ijhe->jhde/dot_general | solution.py:100
  256.8 13.2 %fusion.28 = bf16[80,320,128]{2,1,0:T(8,128)(2,1)} fusion(f32[80,320,512]{2,1,0:T(8,128)} %fusion.40), kind=kLoop, calls=%fused_computation.52 | loop fusion | flops 16384000 | bytes 19660800 | tf_op jit(solution)/shard_map/convert_element_type | solution.py:104
  270.0 13.1 %copy.77 = bf16[80,320,128]{0,2,1:T(8,128)(2,1)} copy(bf16[80,320,128]{2,1,0:T(8,128)(2,1)} %fusion.28) | data formatting | bytes 13107200 | tf_op jit(solution)/shard_map/reshape | solution.py:104
  283.1 305.9 %all-reduce.6.cloned.1.call-done = (bf16[320,4,32]{0,2,1:T(8,128)(2,1)}, bf16[320,4,32,32]{3,2,1,0:T(8,128)(2,1)}) async-done(((bf16[320,4,32]{0,2,1:T(8,128)(2,1)}, bf16[320,4,32,32]{3,2,1,0:T(8,128)(2,1)}), (bf16[320,4,32]{0,2,1:T(8,128)(2,1)}, bf16[320,4,32,32]{3,2,1,0:T(8,128)(2,1)})) %all-reduce.6.cloned.1.call-update) | async-done | bytes 2703376 | tf_op jit(solution)/shard_map/psum | solution.py:108
  590.4 5.5 fusion.57
  596.1 13.9 %multiply_reduce_fusion.1 = (f32[80,320]{0,1:T(8,128)S(1)}, f32[80,320,4,32]{0,3,2,1:T(8,128)}) fusion(f32[80,320,4]{0,2,1:T(4,128)S(1)} %maximum_bitcast_fusion, bf16[320,4,32,32]{3,2,1,0:T(8,128)(2,1)} %get-tuple-element.49, bf16[80,320,4,32]{0,3,2,1:T(8,128)(2,1)} %bitcast.105), kind=kOutput, calls=%fused_computation.28 | convolution fusion | flops 219520000 | bytes 22794240 | tf_op jit(solution)/shard_map/ijhd,jhde->ijhe/dot_general | solution.py:37
  610.1 18.9 %copy.68 = f32[80,320,128]{2,1,0:T(8,128)} copy(f32[80,320,128]{0,2,1:T(8,128)} %bitcast.102) | data formatting | bytes 26214400 | tf_op jit(solution)/shard_map/reshape | solution.py:39
  629.1 9.6 %fusion.38 = bf16[80,320,128]{2,1,0:T(8,128)(2,1)S(1)} fusion(f32[80,320,512]{2,1,0:T(8,128)} %fusion.40, f32[80,320,128]{2,1,0:T(8,128)} %copy.68, f32[128]{0:T(128)S(1)} %copy-done.12, f32[80,320]{1,0:T(8,128)S(1)} %add_rsqrt_fusion.1), kind=kLoop, calls=%fused_computation.69 | loop fusion | flops 22937600 | bytes 32870912 | tf_op jit(solution)/shard_map/convert_element_type | solution.py:41
  641.6 6.4 convert_add_fusion.1
  648.1 97.0 %while.10 = (s32[]{:T(128)}, bf16[10,2560,128]{2,1,0:T(8,128)(2,1)}, f32[10,2560,128]{2,1,0:T(8,128)}, f32[128]{0:T(128)S(1)}, bf16[128,1024]{1,0:T(8,128)(2,1)S(1)}, /*index=5*/bf16[512,128]{1,0:T(8,128)(2,1)S(1)}, s32[]{:T(128)}) while((s32[]{:T(128)}, bf16[10,2560,128]{2,1,0:T(8,128)(2,1)}, f32[10,2560,128]{2,1,0:T(8,128)}, ...), condition=%wide.region_15.16_spmd, body=%wide.region_12.15_spmd.sunk | while | flops 1017448960 | bytes 26046036 | solution.py:125
  652.0 3.4 fusion.84
  (126 shorter events, 101.5 us)
Async XLA Ops:
  7.2 14.8 %copy-start = (bf16[128,512]{1,0:T(8,128)(2,1)S(1)}, bf16[128,512]{1,0:T(8,128)(2,1)}, u32[]{:S(2)}) copy-start(bf16[128,512]{1,0:T(8,128)(2,1)} %param.19) | copy-start | bytes 393220
  7.2 14.8 %copy-start.9 = (f32[128]{0:T(128)S(1)}, f32[128]{0:T(128)}, u32[]{:S(2)}) copy-start(f32[128]{0:T(128)} %param.17) | copy-start | bytes 1540
  7.2 113.0 %all-reduce.4.cloned.1.call-start = ((), (), s32[]{:S(2)}) async-start(), calls=%async_computation | async-start | bytes 5242880 | tf_op jit(solution)/shard_map/psum | solution.py:82
  8.0 5.3 copy-start.2
  87.2 501.9 %all-reduce.6.cloned.1.call-start = ((), (), s32[]{:S(2)}) async-start(), calls=%async_computation.1 | async-start | bytes 21168128 | tf_op jit(solution)/shard_map/psum | solution.py:108
  132.3 14.9 %copy-start.11 = (f32[128]{0:T(128)S(1)}, f32[128]{0:T(128)}, u32[]{:S(2)}) copy-start(f32[128]{0:T(128)} %param.18) | copy-start | bytes 1540
  147.2 9.5 %copy-start.7 = (bf16[128,128]{1,0:T(8,128)(2,1)S(1)}, bf16[128,128]{1,0:T(8,128)(2,1)}, u32[]{:S(2)}) copy-start(bf16[128,128]{1,0:T(8,128)(2,1)} %param.20) | copy-start | bytes 98308
  160.5 19.2 %slice-start = ((s8[6553600]{0:T(1024)(128)(4,1)}), s8[2359296]{0:T(1024)(128)(4,1)S(1)}, s32[]{:S(2)}) async-start(s8[6553600]{0:T(1024)(128)(4,1)} %bitcast.80), calls=%async_computation.2 | async-start | bytes 4718592
  160.5 19.2 %copy-start.5 = (bf16[128,512]{1,0:T(8,128)(2,1)S(1)}, bf16[128,512]{1,0:T(8,128)(2,1)}, u32[]{:S(2)}) copy-start(bf16[128,512]{1,0:T(8,128)(2,1)} %param.23) | copy-start | bytes 393220
  160.5 19.2 %copy-start.10 = (f32[128]{0:T(128)S(1)}, f32[128]{0:T(128)}, u32[]{:S(2)}) copy-start(f32[128]{0:T(128)} %param.21) | copy-start | bytes 1540
  169.5 10.2 %slice-start.1 = ((s8[6553600]{0:T(1024)(128)(4,1)}), s8[4194304]{0:T(1024)(128)(4,1)S(1)}, s32[]{:S(2)}) async-start(s8[6553600]{0:T(1024)(128)(4,1)} %bitcast.80), calls=%async_computation.3 | async-start | bytes 8388608
  610.1 19.0 %copy-start.12 = (f32[128]{0:T(128)S(1)}, f32[128]{0:T(128)}, u32[]{:S(2)}) copy-start(f32[128]{0:T(128)} %param.22) | copy-start | bytes 1540
  610.1 30.8 %slice-start.4 = ((s8[6553600]{0:T(1024)(128)(4,1)}), s8[2359296]{0:T(1024)(128)(4,1)S(1)}, s32[]{:S(2)}) async-start(s8[6553600]{0:T(1024)(128)(4,1)} %bitcast.88), calls=%async_computation.6 | async-start | bytes 4718592
  629.1 9.7 %copy-start.8 = (bf16[128,128]{1,0:T(8,128)(2,1)S(1)}, bf16[128,128]{1,0:T(8,128)(2,1)}, u32[]{:S(2)}) copy-start(bf16[128,128]{1,0:T(8,128)(2,1)} %param.24) | copy-start | bytes 98308
  629.1 11.7 %slice-start.5 = ((s8[6553600]{0:T(1024)(128)(4,1)}), s8[4194304]{0:T(1024)(128)(4,1)S(1)}, s32[]{:S(2)}) async-start(s8[6553600]{0:T(1024)(128)(4,1)} %bitcast.88), calls=%async_computation.7 | async-start | bytes 8388608
  638.7 2.2 slice-start.2
  638.7 2.9 slice-start.3
  640.8 7.3 copy-start.3
  641.6 6.5 copy-start.4
  641.6 6.5 copy-start.6
  641.6 6.5 copy-start.13
  745.1 0.9 copy-start.1
Sparse Core Ops, SparseCore 0:
  87.3 24.9 all-reduce.3
  256.9 332.0 all-reduce.5
where the time goes:
time: 763 us; the launch traced here: 753 us
  waiting for transfers between devices  306 us (40%)
  matrix products  162 us (21%)
  other arithmetic  159 us (21%)
  local copies, waits for them, and re-layouts  107 us (14%)
  between operations  14.9 us (2%)
    psum x1, waiting for transfers between devices, shards(): lax.psum(key_part.astype(jnp.bfloat16), 'col').astype(jnp.float32)  306 us
    reduce_sum x12, other arithmetic, layer_norm(): variance = jnp.mean(centered * centered, axis=-1, keepdims=True)  39.5 us
    dot_general x10, matrix products, transition(): lifted = jnp.dot(normed_block, trans_in, preferred_element_type=jnp.float32)  34.3 us
    reshape x2, local copies, waits for them, and re-layouts, finish(): attended = (numer / denom[..., None]).reshape(gating.shape)  33.7 us
    reduce_sum x12, other arithmetic, layer_norm(): average = jnp.mean(values, axis=-1, keepdims=True)  31.5 us
    convert_element_type x2, other arithmetic, shards(): feature(project[..., :width]).astype(jnp.bfloat16).reshape(head_shape)  26.5 us
    dot_general x2, matrix products, finish(): numer = jnp.einsum(numer_form, query_f, state)  26 us
    dot_general x10, matrix products, transition(): jnp.dot(hidden, trans_out, preferred_element_type=jnp.float32)  24.2 us
  transfers between devices with their start and end apart: 2, of which 1 were waited for; matrix products, arithmetic and copies ran while one was open for 7% of the time, Pallas kernels for 0%

commit v1 on v0

v1 whole, which is shorter than its diff:
```python
import functools
import math

import jax
import jax.numpy as jnp
from jax import lax
from jax.experimental import pallas as pl
from jax.experimental.pallas import tpu as pltpu
from jax.sharding import PartitionSpec as P

HEADS = 4
EPSILON = 1e-05
CHUNKS = 2
BF16 = jnp.bfloat16
F32 = jnp.float32
NT = (((1,), (1,)), ((), ()))


def params():
    return pltpu.CompilerParams(
        dimension_semantics=("arbitrary",), vmem_limit_bytes=56 * 1024 * 1024
    )


def norm(values, gain):
    inverse = 1.0 / values.shape[-1]
    centered = values - jnp.sum(values, axis=-1, keepdims=True) * inverse
    variance = jnp.sum(centered * centered, axis=-1, keepdims=True) * inverse
    return (centered * lax.rsqrt(variance + EPSILON) * gain).astype(BF16)


def feature(values):
    return jnp.where(values > 0, values + 1.0, jnp.exp(values))


def key_state(keys, values, mask_row):
    width = keys.shape[-1]
    depth = width // HEADS
    turned = values.T * mask_row
    ones = jnp.broadcast_to(mask_row, (16, mask_row.shape[-1]))
    full = jnp.dot(jnp.concatenate([turned, ones], axis=0), keys, preferred_element_type=F32)
    lane_head = lax.broadcasted_iota(jnp.int32, (depth, width), 1) // depth
    packed = jnp.zeros((depth, width), F32)
    for head in range(HEADS):
        packed = jnp.where(lane_head == head, full[head * depth : (head + 1) * depth], packed)
    return packed, full[width : width + 1]


def attend(queries, packed, totals, block_mask):
    width = queries.shape[-1]
    depth = width // HEADS
    spread = jnp.concatenate([packed] * HEADS, axis=0)
    right = jnp.concatenate([spread, jnp.broadcast_to(totals, (width, width))], axis=0)
    both = lax.dot_general(queries, right * block_mask, NT, preferred_element_type=F32)
    return both[:, :width] / jnp.maximum(both[:, width:], 1.0)


def head_norm(attended, gain, gate):
    inverse = 1.0 / attended.shape[-1]
    square = jnp.sum(attended * attended, axis=-1, keepdims=True) * inverse
    return attended * lax.rsqrt(square + EPSILON) * gain * gate


def start_kernel(row_mask, pair, col_mask, gain, w_in, query_out, gate_out, state_out, total_out):
    rows, cols, width = pair.shape
    base = pl.program_id(0) * rows
    w = w_in[...]
    for r in range(rows):
        x = norm(pair[r].astype(F32), gain[...])
        project = jnp.dot(x, w, preferred_element_type=F32)
        query_out[r] = feature(project[:, :width]).astype(BF16)
        keys = feature(project[:, width : 2 * width]).astype(BF16)
        values = project[:, 2 * width : 3 * width].astype(BF16)
        gate_out[r] = (jnp.tanh(project[:, 3 * width :]) + 1.0).astype(BF16)
        packed, totals = key_state(keys, values, col_mask[...])
        valid = row_mask[base + r].astype(F32)
        state_out[r] = (packed * valid).astype(BF16)
        total_out[r] = (totals * valid).astype(BF16)


def middle_kernel(
    steps,
    col_mask,
    pair,
    query,
    gate,
    state_a,
    state_b,
    total_a,
    total_b,
    block_mask,
    row_mask,
    head_gain,
    w_out,
    gain,
    w_in,
    *rest,
):
    update_out, query_out, gate_out, state_out, total_out, anchor = rest[-6:]
    block_rows, cols, width = pair.shape
    rows = query_out.shape[1]
    block_cols = query_out.shape[0]
    step = pl.program_id(0)

    @pl.when(step < steps)
    def _():
        for r in range(block_rows):
            packed = (state_a[r].astype(F32) + state_b[r].astype(F32)).astype(BF16)
            totals = (total_a[r].astype(F32) + total_b[r].astype(F32)).astype(BF16)
            attended = attend(query[r], packed, totals, block_mask[...])
            scaled = head_norm(attended, head_gain[...], gate[r].astype(F32)).astype(BF16)
            update = jnp.dot(scaled, w_out[...], preferred_element_type=F32).astype(BF16)
            update_out[r] = update
            first = pair[r].astype(F32) + update.astype(F32)
            anchor[pl.ds((step * block_rows + r) * cols, cols), :] = first

    @pl.when(step >= steps)
    def _():
        base = (step - steps) * block_cols
        w = w_in[...]
        for c in range(block_cols):
            x = norm(anchor[pl.ds(base + c, rows, stride=cols), :], gain[...])
            project = jnp.dot(x, w, preferred_element_type=F32)
            query_out[c] = feature(project[:, :width]).astype(BF16)
            keys = feature(project[:, width : 2 * width]).astype(BF16)
            values = project[:, 2 * width : 3 * width].astype(BF16)
            gate_out[c] = (jnp.tanh(project[:, 3 * width :]) + 1.0).astype(BF16)
            packed, totals = key_state(keys, values, row_mask[...])
            valid = col_mask[base + c].astype(F32)
            state_out[c] = (packed * valid).astype(BF16)
            total_out[c] = (totals * valid).astype(BF16)


def end_kernel(
    pair,
    update_start,
    query,
    gate,
    state,
    total,
    block_mask,
    head_gain,
    w_out,
    gain,
    w_in,
    w_down,
    *rest,
):
    update_out, trans_out, turned = rest[-3:]
    rows, block_cols, width = pair.shape
    hidden = w_down.shape[0]
    for c in range(block_cols):
        attended = attend(query[c], state[c], total[c], block_mask[...])
        scaled = head_norm(attended, head_gain[...], gate[c].astype(F32)).astype(BF16)
        update = jnp.dot(scaled, w_out[...], preferred_element_type=F32)
        turned[pl.ds(c, rows, stride=block_cols), :] = update
    slab = math.gcd(rows, 8)
    for r in range(0, rows, slab):
        update = turned[pl.ds(r * block_cols, slab * block_cols), :].astype(BF16)
        update_out[pl.ds(r, slab)] = update.reshape(slab, block_cols, width)
        first = pair[pl.ds(r, slab)].astype(F32) + update_start[pl.ds(r, slab)].astype(F32)
        second = first.reshape(slab * block_cols, width) + update.astype(F32)
        x = norm(second, gain[...])
        lifted = jnp.dot(x, w_in[...], preferred_element_type=F32)
        half = lifted[:, :hidden]
        inner = (half * (1.0 + jnp.tanh(half)) * lifted[:, hidden:]).astype(BF16)
        down = jnp.dot(inner, w_down[...], preferred_element_type=F32)
        trans_out[pl.ds(r, slab)] = down.reshape(slab, block_cols, width).astype(BF16)


def whole(shape):
    return pl.BlockSpec(shape, lambda *_: (0,) * len(shape), pipeline_mode=pl.Buffered(1))


def shards(
    pair,
    token_mask,
    start_gain,
    start_head_gain,
    start_in,
    start_out,
    end_gain,
    end_head_gain,
    end_in,
    end_out,
    trans_gain,
    trans_in,
    trans_out,
):
    rows, cols, width = pair.shape
    depth = width // HEADS
    hidden = trans_out.shape[0]
    row_ids = lax.dynamic_slice_in_dim(token_mask, lax.axis_index("col") * rows, rows)
    col_ids = lax.dynamic_slice_in_dim(token_mask, lax.axis_index("row") * cols, cols)
    row_line = row_ids.astype(BF16)[None, :]
    col_line = col_ids.astype(BF16)[None, :]
    lanes = jnp.arange(width) // depth
    block_mask = jnp.tile((lanes[:, None] == lanes[None, :]).astype(BF16), (2, 1))
    halve = jnp.where(jnp.arange(4 * width) < 3 * width, 1.0, 0.5).astype(BF16)
    start_w = start_in * halve
    end_w = end_in * halve
    lift_w = trans_in * jnp.where(jnp.arange(2 * hidden) < hidden, 0.5, 1.0).astype(BF16)
    line = lambda gain: gain[None, :]

    tall = math.gcd(rows, 4)
    shape = jax.ShapeDtypeStruct
    block = lambda *dims: pl.BlockSpec(dims, lambda n, *_: (n,) + (0,) * (len(dims) - 1))
    query, gate, state, total = pl.pallas_call(
        start_kernel,
        grid_spec=pltpu.PrefetchScalarGridSpec(
            num_scalar_prefetch=1,
            grid=(rows // tall,),
            in_specs=[
                block(tall, cols, width),
                whole((1, cols)),
                whole((1, width)),
                whole((width, 4 * width)),
            ],
            out_specs=[
                block(tall, cols, width),
                block(tall, cols, width),
                block(tall, depth, width),
                block(tall, 1, width),
            ],
        ),
        out_shape=[
            shape((rows, cols, width), BF16),
            shape((rows, cols, width), BF16),
            shape((rows, depth, width), BF16),
            shape((rows, 1, width), BF16),
        ],
        compiler_params=params(),
        name="start",
    )(row_ids, pair, col_line, line(start_gain), start_w)

    swap = [(n, lax.axis_size("row") - 1 - n) for n in range(lax.axis_size("row"))]
    state_b = lax.ppermute(state, "row", swap)
    total_b = lax.ppermute(total, "row", swap)

    chunk = cols // CHUNKS
    wide = 16
    steps = rows // tall
    turns = chunk // wide

    def middle(part, update):
        low = lambda n: jnp.minimum(n, steps - 1)
        high = lambda n: jnp.maximum(n - steps, 0)
        tile = pl.BlockSpec((tall, chunk, width), lambda n, *_: (low(n), part, 0))
        by_row = lambda *dims: pl.BlockSpec(dims, lambda n, *_: (low(n), 0, 0))
        by_col = lambda *dims: pl.BlockSpec(dims, lambda n, *_: (high(n), 0, 0))
        extra = [] if update is None else [update]
        return pl.pallas_call(
            functools.partial(middle_kernel, steps),
            grid_spec=pltpu.PrefetchScalarGridSpec(
                num_scalar_prefetch=1,
                grid=(steps + turns,),
                in_specs=[
                    tile,
                    tile,
                    tile,
                    by_row(tall, depth, width),
                    by_row(tall, depth, width),
                    by_row(tall, 1, width),
                    by_row(tall, 1, width),
                    whole((2 * width, width)),
                    whole((1, rows)),
                    whole((1, width)),
                    whole((width, width)),
                    whole((1, width)),
                    whole((width, 4 * width)),
                ]
                + [pl.BlockSpec(memory_space=pl.ANY)] * len(extra),
                out_specs=[
                    tile,
                    by_col(wide, rows, width),
                    by_col(wide, rows, width),
                    by_col(wide, depth, width),
                    by_col(wide, 1, width),
                ],
                scratch_shapes=[pltpu.VMEM((rows * chunk, width), F32)],
            ),
            out_shape=[
                shape((rows, cols, width), BF16),
                shape((chunk, rows, width), BF16),
                shape((chunk, rows, width), BF16),
                shape((chunk, depth, width), BF16),
                shape((chunk, 1, width), BF16),
            ],
            input_output_aliases={14: 0} if extra else {},
            compiler_params=params(),
            name="middle",
        )(
            lax.slice_in_dim(col_ids, part * chunk, (part + 1) * chunk),
            pair,
            query,
            gate,
            state,
            state_b,
            total,
            total_b,
            block_mask,
            row_line,
            line(start_head_gain * 0.5),
            start_out,
            line(end_gain),
            end_w,
            *extra,
        )

    def end(part, update_start, parts, outs):
        offset = part * turns
        tile = pl.BlockSpec((rows, wide, width), lambda n: (0, offset + n, 0))
        return pl.pallas_call(
            end_kernel,
            grid=(turns,),
            in_specs=[
                tile,
                tile,
                block(wide, rows, width),
                block(wide, rows, width),
                block(wide, depth, width),
                block(wide, 1, width),
                whole((2 * width, width)),
                whole((1, width)),
                whole((width, width)),
                whole((1, width)),
                whole((width, 2 * hidden)),
                whole((hidden, width)),
            ]
            + [pl.BlockSpec(memory_space=pl.ANY)] * len(outs),
            out_specs=[tile, tile],
            scratch_shapes=[pltpu.VMEM((rows * wide, width), F32)],
            out_shape=[shape((rows, cols, width), BF16)] * 2,
            input_output_aliases={12: 0, 13: 1} if outs else {},
            compiler_params=params(),
            name="end",
        )(
            pair,
            update_start,
            *parts,
            block_mask,
            line(end_head_gain * 0.5),
            end_out,
            line(trans_gain),
            lift_w,
            trans_out,
            *outs,
        )

    update_start = None
    held = []
    for part in range(CHUNKS):
        update_start, query_e, gate_e, state_e, total_e = middle(part, update_start)
        state_e = lax.psum(state_e, "col")
        total_e = lax.psum(total_e, "col")
        held.append((query_e, gate_e, state_e, total_e))
    outs = ()
    for part in range(CHUNKS):
        outs = end(part, update_start, held[part], outs)
    return (update_start, outs[0], outs[1])


def solution(mesh):
    pair_spec = P(("groups", "col"), "row", None)
    return jax.shard_map(
        shards,
        mesh=mesh,
        in_specs=(pair_spec, P("groups")) + (P(),) * 11,
        out_specs=(pair_spec,) * 3,
        check_vma=False,
    )
```

time: 763 us -> 501 us (0.66); the launches traced: 753 us -> 500 us
  Pallas kernels: 0 us -> 286 us
  matrix products: 162 us -> 0 us
  other arithmetic: 159 us -> 5.72 us
  waiting for transfers between devices: 306 us -> 192 us
  local copies, waits for them, and re-layouts: 107 us -> 2.14 us
    pallas_call x0 -> x5, Pallas kernels: none -> 286 us  [the longest x2 132 us: end(): pl.pallas_call(end_kernel, grid=(turns,), in_specs=[tile, tile, block(wid...]
    dot_general x30 -> x0, matrix products: 162 us -> none  [the longest x10 34.3 us: transition(): lifted = jnp.dot(normed_block, trans_in, preferred_element_type=jnp.float32)]
    psum x2, waiting for transfers between devices: 306 us -> 190 us  [the longest x1 120 us: shards(): state_e = lax.psum(state_e, 'col')]
    reduce_sum x26 -> x0, other arithmetic: 106 us -> none  [the longest x12 39.5 us: layer_norm(): variance = jnp.mean(centered * centered, axis=-1, keepdims=True)]
    reshape x5 -> x0, local copies, waits for them, and re-layouts: 72.4 us -> none  [the longest x2 33.7 us: finish(): attended = (numer / denom[..., None]).reshape(gating.shape)]
    convert_element_type x5 -> x4, other arithmetic: 46.3 us -> 0.86 us  [the longest x1 0.77 us: shards(): col_line = col_ids.astype(BF16)[None, :]]
    convert_element_type x2 -> x0, local copies, waits for them, and re-layouts: 20 us -> none  [the longest x1 10.2 us: shards(): feature(project[..., :width]).astype(jnp.bfloat16).reshape(head_shape)]
    slice x1, local copies, waits for them, and re-layouts: 9.79 us -> 0.66 us  [middle(): lax.slice_in_dim(col_ids, part * chunk, (part + 1) * chunk)]
  transfers between devices with their start and end apart: 2 -> 4, of which waited for: 1 -> 3; matrix products, arithmetic and copies ran while one was open for 7% -> 1% of each run, Pallas kernels for 0% -> 0%
where the time goes in v1:
time: 501 us; the launch traced here: 500 us
  Pallas kernels  286 us (57%)
  waiting for transfers between devices  192 us (38%)
  between operations  14.1 us (3%)
  other arithmetic  5.72 us (1%)
    pallas_call x2, Pallas kernels, end(): pl.pallas_call(end_kernel, grid=(turns,), in_specs=[tile, tile, block(wid...  132 us
    psum x1, waiting for transfers between devices, shards(): state_e = lax.psum(state_e, 'col')  120 us
    pallas_call x2, Pallas kernels, middle(): pl.pallas_call(functools.partial(middle_kernel, steps), grid_spec=pltpu.P...  117 us
    psum x1, waiting for transfers between devices, shards(): total_e = lax.psum(total_e, 'col')  70.9 us
    pallas_call x1, Pallas kernels, shards(): pl.pallas_call(start_kernel, grid_spec=pltpu.PrefetchScalarGridSpec(num_s...  37.6 us
  transfers between devices with their start and end apart: 4, of which 3 were waited for; matrix products, arithmetic and copies ran while one was open for 1% of the time, Pallas kernels for 0%

profile of v1, /device:TPU:0, one launch (start us, length us, event | category | flops | bytes accessed | tf_op | source)
XLA Modules:
  0.0 500.3 jit_solution(3235083270997959705)
XLA Ops:
  7.2 0.0 copy-start.3
  7.2 0.0 all-reduce.5.cloned.1.call-start
  7.2 0.8 fusion
  8.0 0.6 broadcast_in_dim.46.col_mask
  8.6 1.3 convert_bitcast_fusion
  9.9 1.7 broadcast_multiply_fusion.1
  11.6 37.6 %start.1 = (bf16[80,320,128]{2,1,0:T(8,128)(2,1)}, bf16[80,320,128]{2,1,0:T(8,128)(2,1)}, bf16[80,32,128]{2,1,0:T(8,128)(2,1)}, bf16[80,1,128]{2,1,0:T(2,128)(2,1)}) custom-call(s32[80]{0:T(128)} %get-tuple-element.44.row_mask, bf16[80,320,128]{2,1,0:T(8,128)(2,1)} %pair.9, bf16[1,320]{1,0:T(2,128)(2,1)} %broadcast_in_dim.46.col_mask, f32[1,128]{1,0:T(1,128)} %bitcast.18, ...), custom_call_target="tpu_custom_call" | custom-call | tf_op jit(solution)/shard_map/start/pallas_call | solution.py:208
  49.2 0.5 collective-permute-start
  49.7 0.1 collective-permute-start.1
  49.8 0.7 fusion.1
  50.5 0.1 compare_convert_fusion
  50.6 0.0 copy-done.3
  50.6 0.6 multiply_bitcast_fusion.1.head_gain
  51.2 0.6 collective-permute-done.1.total_b
  51.7 0.0 collective-permute-done.state_b
  51.7 0.7 tile.21
  52.4 0.0 copy-done.2
  52.4 0.2 copy-done
  52.6 58.3 %middle.2 = (bf16[80,320,128]{2,1,0:T(8,128)(2,1)}, bf16[160,80,128]{2,1,0:T(8,128)(2,1)}, bf16[160,80,128]{2,1,0:T(8,128)(2,1)}, bf16[160,32,128]{2,1,0:T(8,128)(2,1)}, bf16[160,1,128]{2,1,0:T(2,128)(2,1)}) custom-call(s32[160]{0:T(256)} %get-tuple-element.47.col_mask, bf16[80,320,128]{2,1,0:T(8,128)(2,1)} %pair.9, ...), custom_call_target="tpu_custom_call" | custom-call | tf_op jit(solution)/shard_map/middle/pallas_call | solution.py:252
  110.9 0.0 copy-start.4
  110.9 0.0 copy-start.1
  110.9 58.5 %middle.3 = (bf16[80,320,128]{2,1,0:T(8,128)(2,1)}, bf16[160,80,128]{2,1,0:T(8,128)(2,1)}, bf16[160,80,128]{2,1,0:T(8,128)(2,1)}, bf16[160,32,128]{2,1,0:T(8,128)(2,1)}, bf16[160,1,128]{2,1,0:T(2,128)(2,1)}) custom-call(s32[160]{0:T(256)} %get-tuple-element.48.col_mask, bf16[80,320,128]{2,1,0:T(8,128)(2,1)} %pair.9, ...), custom_call_target="tpu_custom_call", output_to_operand_aliasing={{0}: (14, {})} | custom-call | tf_op jit(solution)/shard_map/middle/pallas_call | solution.py:252
  169.4 0.0 all-reduce.5.cloned.1.call-update
  169.4 0.2 all-reduce.7.cloned.1.call-start
  169.6 0.5 all-reduce.7.cloned.1.call-update
  170.2 0.0 copy-done.4
  170.2 0.5 multiply_bitcast_fusion.head_gain
  170.7 0.7 broadcast_multiply_fusion.w_in
  171.5 70.9 %all-reduce.5.cloned.1.call-done = (bf16[160,1,128]{2,1,0:T(2,128)(2,1)}, bf16[160,1,128]{2,1,0:T(2,128)(2,1)}) async-done(((bf16[160,1,128]{2,1,0:T(2,128)(2,1)}, bf16[160,1,128]{2,1,0:T(2,128)(2,1)}), (bf16[160,1,128]{2,1,0:T(2,128)(2,1)}, bf16[160,1,128]{2,1,0:T(2,128)(2,1)})) %all-reduce.5.cloned.1.call-update) | async-done | bytes 81936 | tf_op jit(solution)/shard_map/psum | solution.py:355
  242.3 119.6 %all-reduce.7.cloned.1.call-done = (bf16[160,32,128]{2,1,0:T(8,128)(2,1)}, bf16[160,32,128]{2,1,0:T(8,128)(2,1)}) async-done(((bf16[160,32,128]{2,1,0:T(8,128)(2,1)}, bf16[160,32,128]{2,1,0:T(8,128)(2,1)}), (bf16[160,32,128]{2,1,0:T(8,128)(2,1)}, bf16[160,32,128]{2,1,0:T(8,128)(2,1)})) %all-reduce.7.cloned.1.call-update) | async-done | bytes 2621456 | tf_op jit(solution)/shard_map/psum | solution.py:354
  361.9 65.7 %end.2 = (bf16[80,320,128]{2,1,0:T(8,128)(2,1)}, bf16[80,320,128]{2,1,0:T(8,128)(2,1)}) custom-call(bf16[80,320,128]{2,1,0:T(8,128)(2,1)} %pair.9, bf16[80,320,128]{2,1,0:T(8,128)(2,1)} %get-tuple-element.18.update_start, bf16[160,80,128]{2,1,0:T(8,128)(2,1)} %get-tuple-element.31.query, bf16[160,80,128]{2,1,0:T(8,128)(2,1)} %get-tuple-element.32.gate, ...), custom_call_target="tpu_custom_call" | custom-call | tf_op jit(solution)/shard_map/end/pallas_call | solution.py:313
  427.6 65.8 %end.3 = (bf16[80,320,128]{2,1,0:T(8,128)(2,1)}, bf16[80,320,128]{2,1,0:T(8,128)(2,1)}) custom-call(bf16[80,320,128]{2,1,0:T(8,128)(2,1)} %pair.9, bf16[80,320,128]{2,1,0:T(8,128)(2,1)} %get-tuple-element.18.update_start, bf16[160,80,128]{2,1,0:T(8,128)(2,1)} %get-tuple-element.27.query, ...), custom_call_target="tpu_custom_call", output_to_operand_aliasing={{0}: (12, {}), {1}: (13, {})} | custom-call | tf_op jit(solution)/shard_map/end/pallas_call | solution.py:313
  (6 shorter events, 0.0 us)
Async XLA Ops:
  7.2 43.4 %copy-start.3 = (f32[128]{0:T(128)S(1)}, f32[128]{0:T(128)}, u32[]{:S(2)}) copy-start(f32[128]{0:T(128)} %param.16) | copy-start | bytes 1540
  7.2 235.1 %all-reduce.5.cloned.1.call-start = ((), (), s32[]{:S(2)}) async-start(), calls=%async_computation | async-start | bytes 327680 | tf_op jit(solution)/shard_map/psum | solution.py:355
  49.2 2.5 collective-permute-start
  49.7 2.0 collective-permute-start.1
  51.7 0.7 copy-start.2
  51.7 0.9 copy-start
  110.9 59.3 %copy-start.4 = (f32[128]{0:T(128)S(1)}, f32[128]{0:T(128)}, u32[]{:S(2)}) copy-start(f32[128]{0:T(128)} %param.20) | copy-start | bytes 1540
  110.9 59.8 %copy-start.1 = (bf16[128,1024]{1,0:T(8,128)(2,1)S(1)}, bf16[128,1024]{1,0:T(8,128)(2,1)}, u32[]{:S(2)}) copy-start(bf16[128,1024]{1,0:T(8,128)(2,1)} %param.24) | copy-start | bytes 786436
  169.4 192.5 %all-reduce.7.cloned.1.call-start = ((), (), s32[]{:S(2)}) async-start(), calls=%async_computation.1 | async-start | bytes 5242880 | tf_op jit(solution)/shard_map/psum | solution.py:354
Sparse Core Ops, SparseCore 0:
  169.5 72.7 all-reduce.4
  246.0 115.8 all-reduce.6
